TPU v7x, 512 devices: a whole 4x4x16 slice. The times are simulated.
512 devices in a mesh: req: 32 (over x, y, core), ctx: 16 (over z).
Axes of the slice: x: 4, y: 4, z: 16, core: 2. Of those that a mesh axis runs over, the one named last changes fastest.
Arguments:
- keys: bfloat16 [131072, 1024], P(('req', 'ctx')), parts along dimension 0, may hold values from -8 to 8
- values: bfloat16 [131072, 1024], P(('req', 'ctx')), parts along dimension 0, may hold values from -6 to 6
- obs_queries: bfloat16 [12288, 8192], P(('req', 'ctx')), parts along dimension 0, may hold values from -120 to 120
- dec_queries: bfloat16 [2048, 1, 8192], P(('req', 'ctx')), parts along dimension 0, may hold values from -120 to 120
- kept_blocks: int32 [256, 32], P('req'), parts along dimension 0, may hold values from -1 to 31, as said below
- kept_counts: int32 [256], P('req'), parts along dimension 0, may hold values from 8 to 32
- dec_lengths: int32 [2048], P('req'), parts along dimension 0, may hold values from 128 to 4096
- out_proj: bfloat16 [8192, 4096], P('ctx'), may hold values from -0.5 to 0.5
Outputs:
- pooled: float32 [8, 131072], P(None, ('req', 'ctx')), parts along dimension 1
- decoded: bfloat16 [2048, 1, 4096], P(('req', 'ctx')), parts along dimension 0
There are 32 independent parts, one for each index of `req`. A program takes and returns all parts, laid end to end along the dimension named above; an argument that names none is the same for every part. Nothing has to cross between parts.
Inputs may be any that keep to these rules, and one draw needn't show every extreme that they name: For each KV head g the first kept_counts[g] entries of kept_blocks[g] are distinct block numbers that always include 0 and 31; the later entries are -1.
All inputs are finite; a program needn't handle non-finite values.
Results may differ from a plain program's by a relative error of at most 0.018.
Values may be sent and summed in bfloat16 or wider, within the bound.
No kernel may reach another device: no remote copies, remote signals or barrier semaphores. Data moves between devices by JAX's collectives and lax.ppermute only.
A program may use at most 128 MiB of HBM per device.

v0:
```python
import jax
import jax.numpy as jnp
from jax import lax
from jax.sharding import PartitionSpec as P

H = 64
KVH = 8
HD = 128
BLOCK = 128
OBS = 384
POOL = 7
STEPS = 1


def with_halo(block, sides, width):
    for axis, dim in sides:
        count = lax.axis_size(axis)
        forward = [(i, i + 1) for i in range(count - 1)]
        backward = [(target, source) for source, target in forward]
        low = lax.ppermute(
            lax.slice_in_dim(block, block.shape[dim] - width, None, axis=dim), axis, forward
        )
        high = lax.ppermute(lax.slice_in_dim(block, 0, width, axis=dim), axis, backward)
        block = jnp.concatenate([low, block, high], axis=dim)
    return block


def pick_rows(source_rows, row_ids):
    return source_rows[row_ids]


def shards(keys, values, obs_queries, dec_queries, kept_blocks, kept_counts, dec_lengths, out_proj):
    devices = lax.axis_size("ctx")
    my_index = lax.axis_index("ctx")
    tok_local = keys.shape[0]
    seq_total = tok_local * devices
    kv_local = max(1, KVH // devices)
    copies = max(1, devices // KVH)
    heads_local = H // devices
    heads_per_kv = heads_local // kv_local
    width_kv = kv_local * HD
    width_q = heads_local * HD
    obs_local = obs_queries.shape[0]
    rows_local = dec_queries.shape[0]
    rows_total = rows_local * devices
    scale = HD ** (-0.5)
    query_send = obs_queries.reshape(obs_local, devices, width_q)
    decode_send = dec_queries.reshape(rows_local * STEPS, devices, width_q)

    def spread(source):
        grouped = source.reshape(tok_local, KVH // kv_local, 1, width_kv)
        grouped = jnp.broadcast_to(grouped, (tok_local, KVH // kv_local, copies, width_kv))
        return grouped.reshape(tok_local, devices, width_kv)

    key_mine, value_mine, query_mine, decode_mine = (
        lax.all_to_all(spread(keys), "ctx", split_axis=1, concat_axis=0, tiled=True),
        lax.all_to_all(spread(values), "ctx", split_axis=1, concat_axis=0, tiled=True),
        lax.all_to_all(query_send, "ctx", split_axis=1, concat_axis=0, tiled=True),
        lax.all_to_all(decode_send, "ctx", split_axis=1, concat_axis=0, tiled=True),
    )
    window = query_mine.reshape(OBS, kv_local, heads_per_kv, HD)
    scores = (
        jnp.einsum("ojhd,sjd->jhos", window, key_mine, preferred_element_type=jnp.float32) * scale
    )
    query_place = seq_total - OBS + jnp.arange(OBS, dtype=jnp.int32)
    visible = query_place[:, None] >= jnp.arange(seq_total, dtype=jnp.int32)[None, :]
    scores = jnp.where(visible[None, None], scores, -1e30)
    row_max = jnp.max(scores, axis=3, keepdims=True)
    weights = jnp.where(visible[None, None], jnp.exp(scores - row_max), 0.0)
    probability = weights / jnp.sum(weights, axis=3, keepdims=True)
    column_part = jnp.sum(probability, axis=(1, 2))
    send_back = column_part.reshape(kv_local, devices, tok_local).transpose(1, 0, 2)
    returned = lax.all_to_all(send_back, "ctx", split_axis=0, concat_axis=0, tiled=True)
    column = (
        returned.reshape(KVH // kv_local, copies, kv_local, tok_local)
        .sum(axis=1)
        .reshape(KVH, tok_local)
    )
    half_width = (POOL - 1) // 2
    padded = with_halo(column, (("ctx", 1),), half_width)
    pooled = padded[:, 0:tok_local]
    for offset in range(1, POOL):
        pooled = pooled + padded[:, offset : offset + tok_local]
    pooled = pooled / POOL
    block_count = kept_blocks.shape[1]
    group_start = my_index // copies * kv_local
    blocks_mine = lax.dynamic_slice_in_dim(kept_blocks, group_start, kv_local, 0)
    counts_mine = lax.dynamic_slice_in_dim(kept_counts, group_start, kv_local, 0)
    places = (
        jnp.maximum(blocks_mine, 0)[:, :, None] * BLOCK
        + jnp.arange(BLOCK, dtype=jnp.int32)[None, None, :]
    )
    places = places.reshape(kv_local, block_count * BLOCK)
    slot_valid = jnp.arange(block_count, dtype=jnp.int32)[None, :] < counts_mine[:, None]
    usable = jnp.broadcast_to(slot_valid[:, :, None], (kv_local, block_count, BLOCK)).reshape(
        kv_local, block_count * BLOCK
    )
    key_pick = jax.vmap(pick_rows, in_axes=(1, 0))(key_mine, places)
    value_pick = jax.vmap(pick_rows, in_axes=(1, 0))(value_mine, places)
    row_lengths = jnp.repeat(dec_lengths, STEPS)
    seen = usable[:, None, :] & (places[:, None, :] < row_lengths[None, :, None])
    decode_rows = decode_mine.reshape(rows_total * STEPS, kv_local, heads_per_kv, HD)
    decode_scores = (
        jnp.einsum("rjhd,jkd->jhrk", decode_rows, key_pick, preferred_element_type=jnp.float32)
        * scale
    )
    decode_scores = jnp.where(seen[:, None], decode_scores, -1e30)
    decode_max = jnp.max(decode_scores, axis=3, keepdims=True)
    decode_weights = jnp.where(seen[:, None], jnp.exp(decode_scores - decode_max), 0.0)
    decode_total = jnp.sum(decode_weights, axis=3, keepdims=True)
    rounded = decode_weights.astype(jnp.bfloat16)
    summed = jnp.einsum("jhrk,jkd->jhrd", rounded, value_pick, preferred_element_type=jnp.float32)
    attended = (summed / decode_total).astype(jnp.bfloat16)
    attended_rows = attended.transpose(2, 0, 1, 3).reshape(rows_total, STEPS, width_q)
    product = jnp.dot(
        attended_rows.reshape(rows_local * lax.axis_size("ctx") * STEPS, width_q),
        out_proj,
        preferred_element_type=jnp.float32,
    )
    decoded = lax.psum_scatter(
        product.reshape(rows_local * lax.axis_size("ctx"), STEPS, out_proj.shape[1]).astype(
            jnp.bfloat16
        ),
        "ctx",
        scatter_dimension=0,
        tiled=True,
    )
    return (pooled, decoded)


def solution(mesh):
    return jax.shard_map(
        shards,
        mesh=mesh,
        in_specs=(
            P(("req", "ctx"), None),
            P(("req", "ctx"), None),
            P(("req", "ctx"), None),
            P(("req", "ctx"), None, None),
            P("req", None),
            P("req"),
            P("req"),
            P("ctx", None),
        ),
        out_specs=(P(None, ("req", "ctx")), P(("req", "ctx"), None, None)),
        check_vma=False,
    )
```

profile of v0, /device:TPU:6, one launch (start us, length us, event | category | flops | bytes accessed | tf_op | source)
XLA Modules:
  0.0 362.3 jit_solution(6539565158851182211)
XLA Ops:
  7.2 15.3 %all-to-all-start.3 = ((bf16[4,16,512]{2,0,1:T(4,128)(2,1)}), bf16[4,16,512]{2,0,1:T(4,128)(2,1)S(1)}, u32[]{:S(2)}, u32[]{:S(2)}) async-start(bf16[4,16,512]{2,0,1:T(4,128)(2,1)} %bitcast.120), calls=%async_computation.3 | async-start | bytes 131072 | tf_op jit(solution)/shard_map/all_to_all | solution.py:59
  22.5 1.8 copy.72
  24.3 10.9 %all-to-all-done.3 = bf16[4,16,512]{2,0,1:T(4,128)(2,1)S(1)} async-done(((bf16[4,16,512]{2,0,1:T(4,128)(2,1)}), bf16[4,16,512]{2,0,1:T(4,128)(2,1)S(1)}, u32[]{:S(2)}, u32[]{:S(2)}) %all-to-all-start.3) | async-done | bytes 65568 | tf_op jit(solution)/shard_map/all_to_all | solution.py:59
  35.3 3.6 all-to-all-start.1
  39.0 21.8 %all-to-all-done.1 = bf16[24,16,512]{2,0,1:T(8,128)(2,1)S(1)} async-done(((bf16[24,16,512]{2,0,1:T(8,128)(2,1)}), bf16[24,16,512]{2,0,1:T(8,128)(2,1)S(1)}, u32[]{:S(2)}, u32[]{:S(2)}) %all-to-all-start.1) | async-done | bytes 393248 | tf_op jit(solution)/shard_map/all_to_all | solution.py:58
  61.9 6.6 %all-to-all-start = ((bf16[256,16,128]{2,0,1:T(8,128)(2,1)}), bf16[256,16,128]{2,0,1:T(8,128)(2,1)S(1)}, u32[]{:S(2)}, u32[]{:S(2)}) async-start(bf16[256,16,128]{2,0,1:T(8,128)(2,1)} %bitcast), calls=%async_computation | async-start | bytes 2097152 | tf_op jit(solution)/shard_map/all_to_all | solution.py:56
  70.8 46.9 %all-to-all-done = bf16[256,16,128]{2,0,1:T(8,128)(2,1)S(1)} async-done(((bf16[256,16,128]{2,0,1:T(8,128)(2,1)}), bf16[256,16,128]{2,0,1:T(8,128)(2,1)S(1)}, u32[]{:S(2)}, u32[]{:S(2)}) %all-to-all-start) | async-done | bytes 1048608 | tf_op jit(solution)/shard_map/all_to_all | solution.py:56
  118.9 8.0 %all-to-all-start.4 = ((bf16[256,16,128]{2,0,1:T(8,128)(2,1)}), bf16[256,16,128]{2,0,1:T(8,128)(2,1)S(1)}, u32[]{:S(2)}, u32[]{:S(2)}) async-start(bf16[256,16,128]{2,0,1:T(8,128)(2,1)} %bitcast.115), calls=%async_computation.4 | async-start | bytes 2097152 | tf_op jit(solution)/shard_map/all_to_all | solution.py:57
  127.4 2.4 iota_compare_fusion
  130.6 34.7 %gather_fusion = bf16[4096,128]{1,0:T(8,128)(2,1)} fusion(bf16[1,4096,128]{2,1,0:T(8,128)(2,1)S(1)} %bitcast.112, s32[4096]{0:T(1024)S(1)} %bitcast.110), kind=kCustom, calls=%fused_computation | custom fusion | bytes 2129920 | tf_op jit(solution)/shard_map/vmap()/gather | solution.py:29
  165.3 11.7 %all-to-all-done.4 = bf16[256,16,128]{2,0,1:T(8,128)(2,1)S(1)} async-done(((bf16[256,16,128]{2,0,1:T(8,128)(2,1)}), bf16[256,16,128]{2,0,1:T(8,128)(2,1)S(1)}, u32[]{:S(2)}, u32[]{:S(2)}) %all-to-all-start.4) | async-done | bytes 1048608 | tf_op jit(solution)/shard_map/all_to_all | solution.py:57
  177.0 34.7 %gather_fusion.1 = bf16[4096,128]{1,0:T(8,128)(2,1)} fusion(bf16[1,4096,128]{2,1,0:T(8,128)(2,1)S(1)} %bitcast.114, s32[4096]{0:T(1024)S(1)} %bitcast.111), kind=kCustom, calls=%fused_computation.1 | custom fusion | bytes 2129920 | tf_op jit(solution)/shard_map/vmap()/gather | solution.py:29
  211.6 2.3 fusion.45
  217.1 1.7 fusion.4
  218.8 10.5 %fusion = (f32[4,384]{1,0:T(4,128)S(1)}, f32[4096,384,4]{1,0,2:T(8,128)}) fusion(pred[384,4096]{0,1:T(8,128)(4,1)S(1)} %copy-done.2, bf16[4096,128,1]{1,0,2:T(8,128)(2,1)S(1)} %bitcast.113, bf16[384,4,128]{2,1,0:T(4,128)(2,1)S(1)} %copy-done.6), kind=kOutput, calls=%fused_computation.5 | convolution fusion | flops 1629485568 | bytes 28186624 | tf_op jit(solution)/shard_map/ojhd,sjd->jhos/dot_general | solution.py:63
  229.4 12.0 %fusion.1 = f32[4,384]{1,0:T(4,128)S(1)} fusion(f32[4096,384,4]{1,0,2:T(8,128)} %get-tuple-element.5, f32[4,384]{1,0:T(4,128)S(1)} %get-tuple-element.4, pred[384,4096]{0,1:T(8,128)(4,1)S(1)} %copy-done.2), kind=kLoop, calls=%fused_computation.6 | loop fusion | flops 31455744 | bytes 26750976 | tf_op jit(solution)/shard_map/reduce_sum | solution.py:70
  241.4 3.6 copy-done.1
  244.9 8.1 %divide_reduce_fusion = f32[4096]{0:T(1024)} fusion(f32[4096,384,4]{1,0,2:T(8,128)S(1)} %copy-done.1, f32[4,384]{1,0:T(4,128)S(1)} %fusion.1, f32[4,384]{1,0:T(4,128)S(1)} %get-tuple-element.4, pred[384,4096]{0,1:T(8,128)(4,1)S(1)} %copy-done.2), kind=kLoop, calls=%fused_computation.4 | loop fusion | flops 37744640 | bytes 26767360 | tf_op jit(solution)/shard_map/reduce_sum | solution.py:71
  253.0 7.9 %all-to-all-start.2 = ((f32[16,1,256]{2,1,0:T(1,128)}), f32[16,1,256]{2,1,0:T(1,128)S(1)}, u32[]{:S(2)}, u32[]{:S(2)}) async-start(f32[16,1,256]{2,1,0:T(1,128)} %bitcast.9), calls=%async_computation.2 | async-start | bytes 32768 | tf_op jit(solution)/shard_map/all_to_all | solution.py:73
  262.9 10.5 %all-to-all-done.2 = f32[16,1,256]{2,1,0:T(1,128)S(1)} async-done(((f32[16,1,256]{2,1,0:T(1,128)}), f32[16,1,256]{2,1,0:T(1,128)S(1)}, u32[]{:S(2)}, u32[]{:S(2)}) %all-to-all-start.2) | async-done | bytes 16416 | tf_op jit(solution)/shard_map/all_to_all | solution.py:73
  274.9 4.5 %collective-permute-start = (f32[8,3]{1,0:T(8,128)S(1)}, f32[8,3]{1,0:T(8,128)S(1)}, u32[]{:S(2)}, u32[]{:S(2)}) collective-permute-start(f32[8,3]{1,0:T(8,128)S(1)} %get-tuple-element.2), channel_id=1, source_target_pairs={{0,1},{1,2},{2,3},{3,4},{4,5},{5,6},{6,7},{7,8},{8,9},{9,10},{10,1... | collective-permute-start | bytes 296 | tf_op jit(solution)/shard_map/ppermute | solution.py:20
  279.4 1.3 collective-permute-done
  281.4 72.6 %all-reduce.3.cloned.1.call-done = bf16[64,1,4096]{2,0,1:T(8,128)(2,1)} async-done(((bf16[64,1,4096]{2,0,1:T(8,128)(2,1)}), bf16[64,1,4096]{2,0,1:T(8,128)(2,1)}) %all-reduce.3.cloned.1.call-update) | async-done | bytes 524304
  354.0 1.5 constant_dynamic-slice_fusion
  (48 shorter events, 12.6 us)
Async XLA Ops:
  7.2 31.7 %copy-start = (bf16[256,1024]{1,0:T(8,128)(2,1)S(1)}, bf16[256,1024]{1,0:T(8,128)(2,1)}, u32[]{:S(2)}) copy-start(bf16[256,1024]{1,0:T(8,128)(2,1)} %param.8) | copy-start | bytes 1572868
  7.2 61.4 %copy-start.8 = (s32[8]{0:T(128)S(1)}, s32[8]{0:T(128)}, u32[]{:S(2)}) copy-start(s32[8]{0:T(128)} %param.13) | copy-start | bytes 100
  7.2 63.5 %copy-start.5 = (bf16[256,1024]{1,0:T(8,128)(2,1)S(1)}, bf16[256,1024]{1,0:T(8,128)(2,1)}, u32[]{:S(2)}) copy-start(bf16[256,1024]{1,0:T(8,128)(2,1)} %param.9) | copy-start | bytes 1572868
  7.2 28.1 %all-to-all-start.3 = ((bf16[4,16,512]{2,0,1:T(4,128)(2,1)}), bf16[4,16,512]{2,0,1:T(4,128)(2,1)S(1)}, u32[]{:S(2)}, u32[]{:S(2)}) async-start(bf16[4,16,512]{2,0,1:T(4,128)(2,1)} %bitcast.120), calls=%async_computation.3 | async-start | bytes 131072 | tf_op jit(solution)/shard_map/all_to_all | solution.py:59
  35.3 25.5 %all-to-all-start.1 = ((bf16[24,16,512]{2,0,1:T(8,128)(2,1)}), bf16[24,16,512]{2,0,1:T(8,128)(2,1)S(1)}, u32[]{:S(2)}, u32[]{:S(2)}) async-start(bf16[24,16,512]{2,0,1:T(8,128)(2,1)} %bitcast.109), calls=%async_computation.1 | async-start | bytes 786432 | tf_op jit(solution)/shard_map/all_to_all | solution.py:58
  38.9 88.2 %copy-start.7 = (s32[64]{0:T(128)S(1)}, s32[64]{0:T(128)}, u32[]{:S(2)}) copy-start(s32[64]{0:T(128)} %param.14) | copy-start | bytes 772
  61.9 55.8 %all-to-all-start = ((bf16[256,16,128]{2,0,1:T(8,128)(2,1)}), bf16[256,16,128]{2,0,1:T(8,128)(2,1)S(1)}, u32[]{:S(2)}, u32[]{:S(2)}) async-start(bf16[256,16,128]{2,0,1:T(8,128)(2,1)} %bitcast), calls=%async_computation | async-start | bytes 2097152 | tf_op jit(solution)/shard_map/all_to_all | solution.py:56
  118.9 58.1 %all-to-all-start.4 = ((bf16[256,16,128]{2,0,1:T(8,128)(2,1)}), bf16[256,16,128]{2,0,1:T(8,128)(2,1)S(1)}, u32[]{:S(2)}, u32[]{:S(2)}) async-start(bf16[256,16,128]{2,0,1:T(8,128)(2,1)} %bitcast.115), calls=%async_computation.4 | async-start | bytes 2097152 | tf_op jit(solution)/shard_map/all_to_all | solution.py:57
  126.9 227.1 %all-reduce.3.cloned.1.call-start = ((), (), s32[]{:S(2)}) async-start(), calls=%async_computation.5 | async-start | bytes 1048576
  211.6 3.3 copy-start.4
  214.9 2.2 copy-start.3
  215.9 3.0 copy-start.2
  215.9 3.0 copy-start.6
  229.4 15.6 %copy-start.1 = (f32[4096,384,4]{1,0,2:T(8,128)S(1)}, f32[4096,384,4]{1,0,2:T(8,128)}, u32[]{:S(2)}) copy-start(f32[4096,384,4]{1,0,2:T(8,128)} %get-tuple-element.5) | copy-start | bytes 75497472
  253.0 20.4 %all-to-all-start.2 = ((f32[16,1,256]{2,1,0:T(1,128)}), f32[16,1,256]{2,1,0:T(1,128)S(1)}, u32[]{:S(2)}, u32[]{:S(2)}) async-start(f32[16,1,256]{2,1,0:T(1,128)} %bitcast.9), calls=%async_computation.2 | async-start | bytes 32768 | tf_op jit(solution)/shard_map/all_to_all | solution.py:73
  273.6 5.8 %collective-permute-start.1 = (f32[8,3]{1,0:T(8,128)S(1)}, f32[8,3]{1,0:T(8,128)S(1)}, u32[]{:S(2)}, u32[]{:S(2)}) collective-permute-start(f32[8,3]{1,0:T(8,128)S(1)} %get-tuple-element.3), channel_id=1, source_target_pairs={{1,0},{2,1},{3,2},{4,3},{5,4},{6,5},{7,6},{8,7},{9,8},{10,9},{11,1... | collective-permute-start | bytes 296 | tf_op jit(solution)/shard_map/ppermute | solution.py:23
  274.9 5.9 %collective-permute-start = (f32[8,3]{1,0:T(8,128)S(1)}, f32[8,3]{1,0:T(8,128)S(1)}, u32[]{:S(2)}, u32[]{:S(2)}) collective-permute-start(f32[8,3]{1,0:T(8,128)S(1)} %get-tuple-element.2), channel_id=1, source_target_pairs={{0,1},{1,2},{2,3},{3,4},{4,5},{5,6},{6,7},{7,8},{8,9},{9,10},{10,1... | collective-permute-start | bytes 296 | tf_op jit(solution)/shard_map/ppermute | solution.py:20
Sparse Core Ops, SparseCore 0:
  218.9 135.0 all-reduce.2
where the time goes:
time: 363 us; the launch traced here: 362 us
  waiting for transfers between devices  176 us (48%)
  local copies, waits for them, and re-layouts  82.9 us (23%)
  starting transfers between devices  47.3 us (13%)
  other arithmetic  26 us (7%)
  matrix products  15.4 us (4%)
  between operations  15 us (4%)
    unnamed x2, waiting for transfers between devices  72.6 us
    gather x3, local copies, waits for them, and re-layouts, pick_rows(): return source_rows[row_ids]  69.3 us
    all_to_all x1, waiting for transfers between devices, shards(): lax.all_to_all(spread(keys), 'ctx', split_axis=1, concat_axis=0, tiled=True)  46.9 us
    all_to_all x1, waiting for transfers between devices, shards(): lax.all_to_all(query_send, 'ctx', split_axis=1, concat_axis=0, tiled=True)  21.8 us
    all_to_all x1, starting transfers between devices, shards(): lax.all_to_all(decode_send, 'ctx', split_axis=1, concat_axis=0, tiled=True)  15.3 us
    reduce_sum x1, other arithmetic, shards(): probability = weights / jnp.sum(weights, axis=3, keepdims=True)  12 us
    all_to_all x1, waiting for transfers between devices, shards(): lax.all_to_all(spread(values), 'ctx', split_axis=1, concat_axis=0, tiled=...  11.7 us
    all_to_all x1, waiting for transfers between devices, shards(): lax.all_to_all(decode_send, 'ctx', split_axis=1, concat_axis=0, tiled=True)  10.9 us
  transfers between devices with their start and end apart: 8, of which 7 were waited for; matrix products, arithmetic and copies ran while one was open for 21% of the time, Pallas kernels for 0%

commit v1 on v0

v1 whole, which is shorter than its diff:
```python
import functools

import jax
import jax.numpy as jnp
from jax import lax
from jax.experimental import pallas as pl
from jax.experimental.pallas import tpu as pltpu
from jax.sharding import PartitionSpec as P

H = 64
KVH = 8
HD = 128
GROUP = 8
BLOCK = 128
NB = 32
SEQ = 4096
OBS = 384
POOL = 7
ROWS = 64
DOUT = 4096
N = 16
OBS_L = OBS // N
ROW_L = ROWS // N
HQ = 4
K0 = 0
V0 = 128
Q0 = 256
D0 = Q0 + HQ * OBS_L
CH = D0 + GROUP * ROW_L
EXTRA = 128
FOLD = HD ** (-0.5) * 1.4426950408889634
NEG = -1e30
FAR = 1 << 30
BF = jnp.bfloat16
F32 = jnp.float32
VMEM = pl.BlockSpec(memory_space=pltpu.VMEM)
SMEM = pl.BlockSpec(memory_space=pltpu.SMEM)


def params():
    return pltpu.CompilerParams(vmem_limit_bytes=60 << 20)


def pack_kernel(k_ref, v_ref, q_ref, d_ref, out_ref):
    for dest in range(N):
        head, half = dest // 2, dest % 2
        rows = slice(half * BLOCK, (half + 1) * BLOCK)
        cols = slice(head * HD, (head + 1) * HD)
        out_ref[dest, K0 : K0 + BLOCK, :] = k_ref[rows, cols]
        out_ref[dest, V0 : V0 + BLOCK, :] = v_ref[rows, cols]
        pieces = []
        for h in range(HQ):
            at = (dest * HQ + h) * HD
            pieces.append(q_ref[:, at : at + HD].astype(F32))
        out_ref[dest, Q0:D0, :] = jnp.concatenate(pieces, axis=0).astype(BF)
        pieces = []
        for h in range(GROUP):
            at = (head * GROUP + h) * HD
            pieces.append(d_ref[:, at : at + HD].astype(F32))
        out_ref[dest, D0:CH, :] = jnp.concatenate(pieces, axis=0).astype(BF)


def pack(keys, values, obs, dec):
    return pl.pallas_call(
        pack_kernel,
        out_shape=jax.ShapeDtypeStruct((N, CH, HD), BF),
        in_specs=[VMEM] * 4,
        out_specs=VMEM,
        compiler_params=params(),
        name="pack",
    )(keys, values, obs, dec)


def dot_t(a, b):
    return lax.dot_general(a, b, (((1,), (1,)), ((), ())), preferred_element_type=F32)


DROWS = 128


def decode_kernel(c_ref, r_ref, kept_ref, len_ref, send_ref, keep_ref, stat_ref):
    half = c_ref[0]
    key = r_ref[:, K0 : K0 + BLOCK, :].reshape(N * BLOCK, HD)
    val = r_ref[:, V0 : V0 + BLOCK, :].reshape(N * BLOCK, HD)
    lane = lax.broadcasted_iota(jnp.int32, (DROWS // 2, HD), 1)
    per = DROWS // (GROUP * ROW_L)
    for chunk in range(ROWS * GROUP // DROWS):
        query = r_ref[chunk * per : (chunk + 1) * per, D0:CH, :].reshape(DROWS, HD)
        scores = dot_t(query, key)
        seen = kept_ref[...] < len_ref[chunk * DROWS : (chunk + 1) * DROWS, :]
        scores = jnp.where(seen, scores, NEG)
        top = jnp.max(scores, axis=1, keepdims=True).astype(BF).astype(F32)
        weights = jnp.where(seen, jnp.exp2((scores - top) * FOLD), 0.0)
        total = jnp.sum(weights, axis=1, keepdims=True)
        summed = jnp.dot(weights.astype(BF), val, preferred_element_type=F32)

        def halves(x):
            x = x.reshape(per, 2, HQ * ROW_L, x.shape[1])
            low = x[:, 0].reshape(DROWS // 2, x.shape[3])
            high = x[:, 1].reshape(DROWS // 2, x.shape[3])
            mine = jnp.where(half == 0, low, high)
            other = jnp.where(half == 0, high, low)
            return mine, other

        top_mine, top_other = halves(jnp.broadcast_to(top, (DROWS, HD)))
        total_mine, total_other = halves(jnp.broadcast_to(total, (DROWS, HD)))
        sum_mine, sum_other = halves(summed)
        coarse = total_other.astype(BF).astype(F32)
        stat = jnp.where(
            lane == 0, top_other, jnp.where(lane == 1, coarse, total_other - coarse)
        )
        at = slice(chunk * DROWS // 2, (chunk + 1) * DROWS // 2)
        send_ref[at, 0:HD] = sum_other.astype(BF)
        send_ref[at, HD : 2 * HD] = stat.astype(BF)
        keep_ref[at, :] = sum_mine
        stat_ref[at, :] = jnp.where(lane == 0, top_mine, total_mine)


def decode(half, received, kept, lens):
    rows = ROWS * HQ
    return pl.pallas_call(
        decode_kernel,
        out_shape=(
            jax.ShapeDtypeStruct((rows, 2 * HD), BF),
            jax.ShapeDtypeStruct((rows, HD), F32),
            jax.ShapeDtypeStruct((rows, HD), F32),
        ),
        in_specs=[SMEM, VMEM, VMEM, VMEM],
        out_specs=(VMEM, VMEM, VMEM),
        compiler_params=params(),
        name="decode",
    )(half, received, kept, lens)


def project_kernel(other_ref, keep_ref, stat_ref, w_ref, out_ref):
    rows = ROWS * HQ
    other = other_ref[...].astype(F32)
    top_o = other[:, HD : HD + 1]
    total_o = other[:, HD + 1 : HD + 2] + other[:, HD + 2 : HD + 3]
    top_m = stat_ref[:, 0:1]
    total_m = stat_ref[:, 1:2]
    top = jnp.maximum(top_o, top_m)
    fac_o = jnp.exp2((top_o - top) * FOLD)
    fac_m = jnp.exp2((top_m - top) * FOLD)
    total = total_o * fac_o + total_m * fac_m
    mixed = other[:, 0:HD] * fac_o + keep_ref[...] * fac_m
    attended = (mixed / total).astype(BF)
    out_row = lax.broadcasted_iota(jnp.int32, (ROWS, rows), 0)
    in_row = lax.broadcasted_iota(jnp.int32, (ROWS, rows), 1)
    base = (out_row >> 2) * (HQ * ROW_L) + (out_row & 3)
    parts = []
    for h in range(HQ):
        pick = jnp.where(in_row == base + h * ROW_L, 1.0, 0.0).astype(BF)
        parts.append(jnp.dot(pick, attended, preferred_element_type=F32).astype(BF))
    flat = jnp.concatenate(parts, axis=1)
    step = 512
    for col in range(0, DOUT, step):
        product = jnp.dot(flat, w_ref[:, col : col + step], preferred_element_type=F32)
        for dest in range(N):
            out_ref[dest, :, col : col + step] = product[
                dest * ROW_L : (dest + 1) * ROW_L, :
            ].astype(BF)


def project(other, keep, stat, w):
    return pl.pallas_call(
        project_kernel,
        out_shape=jax.ShapeDtypeStruct((N, ROW_L, DOUT), BF),
        in_specs=[VMEM] * 4,
        out_specs=VMEM,
        compiler_params=params(),
        name="project",
    )(other, keep, stat, w)


WSRC = 4
WROWS = WSRC * HQ * OBS_L


def window_kernel(c_ref, r_ref, x_ref, out_ref, s_ref, acc_ref):
    half = c_ref[0]
    acc_ref[...] = jnp.zeros_like(acc_ref)
    row = lax.broadcasted_iota(jnp.int32, (WROWS, BLOCK), 0)
    lane = lax.broadcasted_iota(jnp.int32, (WROWS, BLOCK), 1)
    local = (row // (HQ * OBS_L)) * OBS_L + row % OBS_L
    diff = lane - local
    for chunk in range(N // WSRC):
        query = r_ref[chunk * WSRC : (chunk + 1) * WSRC, Q0:D0, :].reshape(WROWS, HD)
        place = SEQ - OBS + chunk * WSRC * OBS_L
        peak = None
        for side in range(2):
            parity = half if side == 0 else 1 - half
            for pair in range(N // 2):
                if side == 0:
                    key = r_ref[2 * pair : 2 * pair + 2, K0 : K0 + BLOCK, :]
                else:
                    key = x_ref[2 * pair : 2 * pair + 2]
                scores = dot_t(query, key.reshape(2 * BLOCK, HD))
                if pair == N // 2 - 1:
                    shown = []
                    for j in range(2):
                        start = (2 * (2 * pair + j) + parity) * BLOCK
                        part = scores[:, j * BLOCK : (j + 1) * BLOCK]
                        shown.append(jnp.where(diff <= place - start, part, NEG))
                    scores = jnp.concatenate(shown, axis=1)
                at = (side * (N // 2) + pair) * 2 * BLOCK
                s_ref[:, at : at + 2 * BLOCK] = scores
                best = jnp.maximum(scores[:, 0:BLOCK], scores[:, BLOCK:])
                peak = best if peak is None else jnp.maximum(peak, best)
        top = jnp.max(peak, axis=1, keepdims=True) * FOLD
        total = jnp.zeros((WROWS, BLOCK), F32)
        for b in range(NB):
            at = slice(b * BLOCK, (b + 1) * BLOCK)
            weight = jnp.exp2(s_ref[:, at] * FOLD - top)
            s_ref[:, at] = weight
            total = total + weight
        share = 1.0 / jnp.sum(total, axis=1, keepdims=True)
        share = jnp.broadcast_to(share, (WROWS, BLOCK))
        for b in range(NB):
            at = slice(b * BLOCK, (b + 1) * BLOCK)
            part = s_ref[:, at] * share
            acc_ref[b] += jnp.sum(part.reshape(WROWS // 8, 8, BLOCK), axis=0)
    sums = jnp.sum(acc_ref[...], axis=1)
    mine, other = sums[0:N], sums[N:NB]
    out_ref[0] = jnp.where(half == 0, mine, other)
    out_ref[1] = jnp.where(half == 0, other, mine)


def window(half, received, partner):
    return pl.pallas_call(
        window_kernel,
        out_shape=jax.ShapeDtypeStruct((2, N, BLOCK), F32),
        in_specs=[SMEM, VMEM, VMEM],
        out_specs=VMEM,
        scratch_shapes=[
            pltpu.VMEM((WROWS, SEQ), F32),
            pltpu.VMEM((NB, 8, BLOCK), F32),
        ],
        compiler_params=params(),
        name="window",
    )(half, received, partner)


def shards(keys, values, obs_queries, dec_queries, kept_blocks, kept_counts, dec_lengths, out_proj):
    me = lax.axis_index("ctx")
    half = lax.rem(me, 2)
    head = me // 2
    swap = [(i, i ^ 1) for i in range(N)]
    half_arg = half[None].astype(jnp.int32)

    sent = pack(keys, values, obs_queries, dec_queries.reshape(ROW_L, H * HD))
    received = lax.all_to_all(sent, "ctx", 0, 0, tiled=True)
    partner = lax.ppermute(received[:, K0 : K0 + BLOCK, :], "ctx", swap)

    blocks = lax.dynamic_slice_in_dim(kept_blocks, head, 1, 0)
    count = lax.dynamic_slice_in_dim(kept_counts, head, 1, 0)
    mine = 2 * jnp.arange(N, dtype=jnp.int32) + half
    named = (blocks == mine[:, None]) & (jnp.arange(NB, dtype=jnp.int32)[None, :] < count)
    hit = jnp.any(named, axis=1)
    places = mine[:, None] * BLOCK + jnp.arange(BLOCK, dtype=jnp.int32)[None, :]
    kept = jnp.where(hit[:, None], places, FAR).reshape(1, N * BLOCK)
    lens = jnp.broadcast_to(dec_lengths.reshape(N, 1, ROW_L), (N, GROUP, ROW_L))
    lens = lens.reshape(N * GROUP * ROW_L, 1)

    send, keep, stat = decode(half_arg, received, kept, lens)
    other = lax.ppermute(send, "ctx", swap)
    product = project(other, keep, stat, out_proj)

    sums = window(half_arg, received, partner)
    low, high = sums[0], sums[1]
    reach = (POOL - 1) // 2
    edge = jnp.zeros((1, reach), F32)
    left = jnp.concatenate([edge, high[:-1, BLOCK - reach :]], axis=0)
    right = jnp.concatenate([low[1:, :reach], edge], axis=0)
    halo = jnp.concatenate([left, right, jnp.zeros((N, BLOCK - 2 * reach), F32)], axis=1)
    cols = jnp.stack([low, high, halo, jnp.zeros_like(low)], axis=1).astype(BF)
    both = jnp.concatenate([product, cols], axis=2)
    back = lax.all_to_all(both, "ctx", 0, 0, tiled=True)
    decoded = jnp.sum(back[:, :, :DOUT].astype(F32), axis=0).astype(BF)
    column = back[:, :, DOUT:].astype(F32).reshape(KVH, 2, ROW_L, BLOCK).sum(axis=1)
    padded = jnp.concatenate(
        [column[:, 2, :reach], column[:, 0], column[:, 1], column[:, 2, reach : 2 * reach]], axis=1
    )
    width = 2 * BLOCK
    pooled = padded[:, 0:width]
    for offset in range(1, POOL):
        pooled = pooled + padded[:, offset : offset + width]
    pooled = pooled / POOL
    return pooled, decoded[:, None, :]


def solution(mesh):
    return jax.shard_map(
        shards,
        mesh=mesh,
        in_specs=(
            P(("req", "ctx"), None),
            P(("req", "ctx"), None),
            P(("req", "ctx"), None),
            P(("req", "ctx"), None, None),
            P("req", None),
            P("req"),
            P("req"),
            P("ctx", None),
        ),
        out_specs=(P(None, ("req", "ctx")), P(("req", "ctx"), None, None)),
        check_vma=False,
    )
```

time: 363 us -> 171 us (0.47)
  waiting for transfers between devices: 176 us -> 76.7 us
  local copies, waits for them, and re-layouts: 82.9 us -> 4.08 us
  blocking collectives: 0 us -> 41.3 us
  starting transfers between devices: 47.3 us -> 21.3 us
  Pallas kernels: 0 us -> 23.2 us
  other arithmetic: 26 us -> 3.53 us
  matrix products: 15.4 us -> 0 us
  between operations: 15 us -> 0.77 us
    unnamed x2 -> x0, waiting for transfers between devices: 72.6 us -> none
    gather x3 -> x0, local copies, waits for them, and re-layouts: 69.3 us -> none  [pick_rows(): return source_rows[row_ids]]
    all_to_all x0 -> x1, blocking collectives: none -> 41.3 us  [shards(): back = lax.all_to_all(both, 'ctx', 0, 0, tiled=True)]
    all_to_all x5 -> x1, waiting for transfers between devices: 102 us -> 73.6 us  [shards(): received = lax.all_to_all(sent, 'ctx', 0, 0, tiled=True)]
    all_to_all x5 -> x1, starting transfers between devices: 41.4 us -> 15.3 us  [shards(): received = lax.all_to_all(sent, 'ctx', 0, 0, tiled=True)]
    pallas_call x0 -> x4, Pallas kernels: none -> 23.2 us  [the longest x1 11.4 us: window(): pl.pallas_call(window_kernel, out_shape=jax.ShapeDtypeStruct((2, N, BLOCK...]
    reduce_sum x4 -> x2, other arithmetic: 21.1 us -> 0.85 us  [the longest x1 0.83 us: shards(): decoded = jnp.sum(back[:, :, :DOUT].astype(F32), axis=0).astype(BF)]
    dot_general x4 -> x0, matrix products: 15.4 us -> none  [the longest x1 10.5 us: shards(): jnp.einsum('ojhd,sjd->jhos', window, key_mine, preferred_element_type=jnp...]
  transfers between devices with their start and end apart: 8 -> 3, of which waited for: 7 -> 2; matrix products, arithmetic and copies ran while one was open for 21% -> 2% of each run, Pallas kernels for 0% -> 5%
where the time goes in v1:
time: 171 us
  waiting for transfers between devices  76.7 us (45%)
  blocking collectives  41.3 us (24%)
  Pallas kernels  23.2 us (14%)
  starting transfers between devices  21.3 us (12%)
  local copies, waits for them, and re-layouts  4.08 us (2%)
  other arithmetic  3.53 us (2%)
    all_to_all x1, waiting for transfers between devices, shards(): received = lax.all_to_all(sent, 'ctx', 0, 0, tiled=True)  73.6 us
    all_to_all x1, blocking collectives, shards(): back = lax.all_to_all(both, 'ctx', 0, 0, tiled=True)  41.3 us
    all_to_all x1, starting transfers between devices, shards(): received = lax.all_to_all(sent, 'ctx', 0, 0, tiled=True)  15.3 us
    pallas_call x1, Pallas kernels, window(): pl.pallas_call(window_kernel, out_shape=jax.ShapeDtypeStruct((2, N, BLOCK...  11.4 us
    pallas_call x1, Pallas kernels, decode(): pl.pallas_call(decode_kernel, out_shape=(jax.ShapeDtypeStruct((rows, 2 *...  4.71 us
    pallas_call x1, Pallas kernels, project(): pl.pallas_call(project_kernel, out_shape=jax.ShapeDtypeStruct((N, ROW_L,...  4.43 us
    ppermute x1, starting transfers between devices, shards(): other = lax.ppermute(send, 'ctx', swap)  3.8 us
  transfers between devices with their start and end apart: 3, of which 2 were waited for; matrix products, arithmetic and copies ran while one was open for 2% of the time, Pallas kernels for 5%

profile of v1, /device:TPU:6, one launch (start us, length us, event | category | flops | bytes accessed | tf_op | source)
XLA Modules:
  0.0 170.9 jit_solution(6639521076401354087)
XLA Ops:
  0.6 2.7 %pack.1 = bf16[16,384,128]{2,1,0:T(8,128)(2,1)} custom-call(bf16[256,1024]{1,0:T(8,128)(2,1)} %k_ref.1, bf16[256,1024]{1,0:T(8,128)(2,1)} %v_ref.1, bf16[24,8192]{1,0:T(8,128)(2,1)} %q_ref.1, bf16[4,8192]{1,0:T(4,128)(2,1)} %bitcast.27), custom_call_target="tpu_custom_call" | custom-call | tf_op jit(solution)/shard_map/pack/pallas_call | solution.py:64
  3.4 15.3 %all-to-all-start = ((bf16[16,384,128]{2,1,0:T(8,128)(2,1)}), bf16[16,384,128]{2,1,0:T(8,128)(2,1)S(1)}, u32[]{:S(2)}, u32[]{:S(2)}) async-start(bf16[16,384,128]{2,1,0:T(8,128)(2,1)} %pack.1), calls=%async_computation | async-start | bytes 3145728 | tf_op jit(solution)/shard_map/all_to_all | solution.py:252
  18.7 0.6 dynamic_slice.7
  19.4 73.6 %all-to-all-done.r_ref = bf16[16,384,128]{2,1,0:T(8,128)(2,1)S(1)} async-done(((bf16[16,384,128]{2,1,0:T(8,128)(2,1)}), bf16[16,384,128]{2,1,0:T(8,128)(2,1)S(1)}, u32[]{:S(2)}, u32[]{:S(2)}) %all-to-all-start) | async-done | bytes 1572896 | tf_op jit(solution)/shard_map/all_to_all | solution.py:252
  93.0 2.2 %collective-permute-start.1 = (bf16[16,128,128]{2,1,0:T(8,128)(2,1)S(1)}, bf16[16,128,128]{2,1,0:T(8,128)(2,1)S(1)}, u32[]{:S(2)}, u32[]{:S(2)}) collective-permute-start(bf16[16,128,128]{2,1,0:T(8,128)(2,1)S(1)} %slice.78), channel_id=1, source_target_pairs={{0,1},{1,0},{2,3},{3,2},{4,5},{5,4},{6,7},{7,6},{8,9},{9,8},{10,11... | collective-permute-start | bytes 1572872 | tf_op jit(solution)/shard_map/ppermute | solution.py:253
  95.2 0.7 iota_compare_fusion.3
  95.9 0.1 broadcast_in_dim.37
  96.0 0.8 reshape.79.len_ref
  96.8 0.2 and_reduce_fusion
  97.0 0.7 add_select_fusion
  97.7 4.7 %decode.1 = (bf16[256,256]{1,0:T(8,128)(2,1)}, f32[256,128]{1,0:T(8,128)}, f32[256,128]{1,0:T(8,128)}) custom-call(s32[1]{0:T(128)} %bitcast.c_ref, bf16[16,384,128]{2,1,0:T(8,128)(2,1)} %copy-done.1, s32[1,2048]{1,0:T(1,128)} %bitcast.32, s32[512,1]{1,0:T(8,128)} %reshape.79.len_ref), custom_call_target="tpu_custom_call" | custom-call | tf_op jit(solution)/shard_map/decode/pallas_call | solution.py:121
  102.4 3.8 %collective-permute-start = (bf16[256,256]{1,0:T(8,128)(2,1)}, bf16[256,256]{1,0:T(8,128)(2,1)S(1)}, u32[]{:S(2)}, u32[]{:S(2)}) collective-permute-start(bf16[256,256]{1,0:T(8,128)(2,1)} %get-tuple-element.5), channel_id=1, source_target_pairs={{0,1},{1,0},{2,3},{3,2},{4,5},{5,4},{6,7},{7,6},{8,9},{9,8},{10,11... | collective-permute-start | bytes 393224 | tf_op jit(solution)/shard_map/ppermute | solution.py:266
  106.3 3.1 %collective-permute-done.other_ref = bf16[256,256]{1,0:T(8,128)(2,1)S(1)} collective-permute-done((bf16[256,256]{1,0:T(8,128)(2,1)}, bf16[256,256]{1,0:T(8,128)(2,1)S(1)}, u32[]{:S(2)}, u32[]{:S(2)}) %collective-permute-start) | collective-permute-done | bytes 131104 | tf_op jit(solution)/shard_map/ppermute | solution.py:266
  109.4 0.7 copy-done.4
  110.1 4.4 %project.1 = bf16[16,4,4096]{2,1,0:T(4,128)(2,1)} custom-call(bf16[256,256]{1,0:T(8,128)(2,1)} %copy-done.4, f32[256,128]{1,0:T(8,128)} %get-tuple-element.6.keep_ref, f32[256,128]{1,0:T(8,128)} %get-tuple-element.7.stat_ref, bf16[512,4096]{1,0:T(8,128)(2,1)} %w_ref.1), custom_call_target="tpu_custom_call" | custom-call | tf_op jit(solution)/shard_map/project/pallas_call | solution.py:166
  114.5 0.8 copy-done.3
  115.3 11.4 %window.1 = f32[2,16,128]{2,1,0:T(8,128)} custom-call(s32[1]{0:T(128)} %bitcast.c_ref, bf16[16,384,128]{2,1,0:T(8,128)(2,1)} %copy-done.1, bf16[16,128,128]{2,1,0:T(8,128)(2,1)} %copy-done.3), custom_call_target="tpu_custom_call" | custom-call | tf_op jit(solution)/shard_map/window/pallas_call | solution.py:230
  126.7 0.7 fusion.9
  127.5 0.1 fusion.7
  127.6 0.1 maximum_maximum_fusion
  127.7 0.2 pad_maximum_fusion
  127.9 41.3 %all_to_all.10 = bf16[16,4,4224]{2,1,0:T(4,128)(2,1)S(1)} all-to-all(bf16[16,4,4224]{2,1,0:T(4,128)(2,1)S(1)} %pad_maximum_fusion), channel_id=1, replica_groups=mesh['req'=32,'ctx'=16] {'ctx'}, dimensions={0} | all-to-all | bytes 1081344 | tf_op jit(solution)/shard_map/all_to_all | solution.py:278
  169.4 0.7 fusion
  170.1 0.8 slice_reduce_fusion
  (27 shorter events, 0.5 us)
Async XLA Ops:
  0.6 18.7 %copy-start = (s32[8,32]{1,0:T(8,128)S(1)}, s32[8,32]{1,0:T(8,128)}, u32[]{:S(2)}) copy-start(s32[8,32]{1,0:T(8,128)} %param.12) | copy-start | bytes 3076
  3.4 15.4 %copy-start.6 = (s32[8]{0:T(128)S(1)}, s32[8]{0:T(128)}, u32[]{:S(2)}) copy-start(s32[8]{0:T(128)} %param.13) | copy-start | bytes 100
  3.4 92.5 %copy-start.5 = (s32[64]{0:T(128)S(1)}, s32[64]{0:T(128)}, u32[]{:S(2)}) copy-start(s32[64]{0:T(128)} %param.14) | copy-start | bytes 772
  3.4 89.6 %all-to-all-start = ((bf16[16,384,128]{2,1,0:T(8,128)(2,1)}), bf16[16,384,128]{2,1,0:T(8,128)(2,1)S(1)}, u32[]{:S(2)}, u32[]{:S(2)}) async-start(bf16[16,384,128]{2,1,0:T(8,128)(2,1)} %pack.1), calls=%async_computation | async-start | bytes 3145728 | tf_op jit(solution)/shard_map/all_to_all | solution.py:252
  92.9 4.7 %copy-start.1 = (bf16[16,384,128]{2,1,0:T(8,128)(2,1)}, bf16[16,384,128]{2,1,0:T(8,128)(2,1)S(1)}, u32[]{:S(2)}) copy-start(bf16[16,384,128]{2,1,0:T(8,128)(2,1)S(1)} %all-to-all-done.r_ref) | copy-start | bytes 4718596
  93.0 21.5 %collective-permute-start.1 = (bf16[16,128,128]{2,1,0:T(8,128)(2,1)S(1)}, bf16[16,128,128]{2,1,0:T(8,128)(2,1)S(1)}, u32[]{:S(2)}, u32[]{:S(2)}) collective-permute-start(bf16[16,128,128]{2,1,0:T(8,128)(2,1)S(1)} %slice.78), channel_id=1, source_target_pairs={{0,1},{1,0},{2,3},{3,2},{4,5},{5,4},{6,7},{7,6},{8,9},{9,8},{10,11... | collective-permute-start | bytes 1572872 | tf_op jit(solution)/shard_map/ppermute | solution.py:253
  102.4 7.1 %collective-permute-start = (bf16[256,256]{1,0:T(8,128)(2,1)}, bf16[256,256]{1,0:T(8,128)(2,1)S(1)}, u32[]{:S(2)}, u32[]{:S(2)}) collective-permute-start(bf16[256,256]{1,0:T(8,128)(2,1)} %get-tuple-element.5), channel_id=1, source_target_pairs={{0,1},{1,0},{2,3},{3,2},{4,5},{5,4},{6,7},{7,6},{8,9},{9,8},{10,11... | collective-permute-start | bytes 393224 | tf_op jit(solution)/shard_map/ppermute | solution.py:266
  109.4 0.7 copy-start.4
  114.5 13.2 %copy-start.2 = (bf16[16,4,4096]{2,1,0:T(4,128)(2,1)S(1)}, bf16[16,4,4096]{2,1,0:T(4,128)(2,1)}, u32[]{:S(2)}) copy-start(bf16[16,4,4096]{2,1,0:T(4,128)(2,1)} %project.1) | copy-start | bytes 1572868
  114.5 0.8 copy-start.3
